TPU v7x, 256 devices: a whole 4x4x8 slice. The times are simulated.
256 devices in a mesh: seg: 64 (over z, x, core), head: 4 (over y).
Axes of the slice: x: 4, y: 4, z: 8, core: 2. Of those that a mesh axis runs over, the one named last changes fastest.
Arguments:
- queries: bfloat16 [16384, 1536], P(('seg', 'head')), may hold values from -8 to 8
- key_rows: bfloat16 [16384, 1536], P(('seg', 'head')), may hold values from -8 to 8
- value_rows: bfloat16 [16384, 1536], P(('seg', 'head')), may hold values from -6 to 6
- w_first: float32 [24, 64, 256], P('head'), may hold values from -0.75 to 0.75
- w_second: float32 [24, 256, 64], P('head'), may hold values from -0.375 to 0.375
- gate_pairs: float32 [2, 1536], P(None, 'head'), may hold values from 0.3 to 1.5
Outputs:
- mixed: float32 [16384, 1536], P('seg', 'head')
All inputs are finite; a program needn't handle non-finite values.
Results may differ from a plain program's by a relative error of at most 0.0011.
Values may be sent and summed in bfloat16 or wider, within the bound.
A program may use at most 128 MiB of HBM per device.

v0:
```python
import jax
import jax.numpy as jnp
from jax import lax
from jax.sharding import PartitionSpec as P

HEAD_DIM = 64
GROUP = 8


inner_rate = 0.05
norm_epsilon = 1e-05
highest = lax.Precision.HIGHEST


def swapped(value, axis, stride):
    mask = 2**stride
    pairs = [(source, source ^ mask) for source in range(lax.axis_size(axis))]
    return lax.ppermute(value, axis, pairs)


def entering(shard, axis, combine, identity):
    size, position = (lax.axis_size(axis), lax.axis_index(axis))
    everything = jax.tree.map(lambda part: lax.all_gather(part, axis), shard)
    start = jax.tree.map(
        lambda part, zero: jnp.broadcast_to(jnp.asarray(zero, part.dtype), part.shape),
        shard,
        identity,
    )

    def lap(k, before):
        reached = k < position
        new = combine(before, jax.tree.map(lambda part: part[k], everything))
        return jax.tree.map(lambda a, b: jnp.where(reached, a, b), new, before)

    return lax.fori_loop(0, size, lap, start)


def inner_model(inputs, first, second):
    hidden = jnp.einsum("nhd,hdf->nhf", inputs, first, precision=highest)
    mapped = jnp.einsum("nhf,hfd->nhd", jax.nn.gelu(hidden), second, precision=highest)
    centre = mapped - jnp.mean(mapped, axis=-1, keepdims=True)
    spread = jnp.mean(centre * centre, axis=-1, keepdims=True)
    return centre * lax.rsqrt(spread + norm_epsilon)


def inner_loss(first, second, inputs, target):
    error = inner_model(inputs, first, second) - target
    return 0.5 * jnp.sum(error * error) / inputs.shape[0]


def segment_attention(query_rows, key_block, value_block):
    head_count = query_rows.shape[1] // HEAD_DIM

    def head_step(head_index, result):
        start = head_index * HEAD_DIM
        head_query = lax.dynamic_slice_in_dim(query_rows, start, HEAD_DIM, 1)
        head_key = lax.dynamic_slice_in_dim(key_block, start, HEAD_DIM, 1)
        head_value = lax.dynamic_slice_in_dim(value_block, start, HEAD_DIM, 1)
        scores = lax.dot_general(
            head_query, head_key, (((1,), (1,)), ((), ())), preferred_element_type=jnp.float32
        ) * HEAD_DIM ** (-0.5)
        scores = scores - jnp.max(scores, axis=-1, keepdims=True)
        expon = jnp.exp(scores)
        weights = (expon / jnp.sum(expon, axis=-1, keepdims=True)).astype(jnp.bfloat16)
        attended = jnp.dot(weights, head_value, preferred_element_type=jnp.float32)
        return lax.dynamic_update_slice_in_dim(result, attended, start, 1)

    return lax.fori_loop(0, head_count, head_step, jnp.zeros(query_rows.shape, jnp.float32))


def add_pair(earlier, later):
    return (earlier[0] + later[0], earlier[1] + later[1])


def on_device(queries, key_rows, value_rows, w_first, w_second, gate_pairs):
    query_here, key_here, value_here = (
        lax.all_to_all(queries, "head", split_axis=1, concat_axis=0, tiled=True),
        lax.all_to_all(key_rows, "head", split_axis=1, concat_axis=0, tiled=True),
        lax.all_to_all(value_rows, "head", split_axis=1, concat_axis=0, tiled=True),
    )
    row_count, width = query_here.shape
    heads_here = width // HEAD_DIM
    segment_keys, segment_values = (key_here, value_here)
    for bit_index in range(GROUP.bit_length() - 1):
        other_keys, other_values = swapped((segment_keys, segment_values), "seg", bit_index)
        segment_keys = jnp.concatenate([segment_keys, other_keys], axis=0)
        segment_values = jnp.concatenate([segment_values, other_values], axis=0)
    attention = segment_attention(query_here, segment_keys, segment_values)
    inputs = key_here.astype(jnp.float32).reshape(row_count, heads_here, HEAD_DIM)
    target = value_here.astype(jnp.float32).reshape(row_count, heads_here, HEAD_DIM) - inputs
    grad_first, grad_second = jax.grad(inner_loss, argnums=(0, 1))(
        w_first, w_second, inputs, target
    )
    zero_pair = (jnp.zeros_like(grad_first), jnp.zeros_like(grad_second))
    before_first, before_second = entering((grad_first, grad_second), "seg", add_pair, zero_pair)
    ahead_first = before_first + grad_first
    ahead_second = before_second + grad_second
    total_first, total_second = lax.psum((grad_first, grad_second), "seg")
    behind_first = total_first - before_first
    behind_second = total_second - before_second
    query_float = query_here.astype(jnp.float32).reshape(row_count, heads_here, HEAD_DIM)
    forward_out = query_float + inner_model(
        query_float, w_first - inner_rate * ahead_first, w_second - inner_rate * ahead_second
    )
    backward_out = query_float + inner_model(
        query_float, w_first - inner_rate * behind_first, w_second - inner_rate * behind_second
    )
    gate_forward = jnp.tanh(gate_pairs[0])
    gate_backward = jnp.tanh(gate_pairs[1])
    return (
        attention
        + gate_forward * forward_out.reshape(row_count, width)
        + gate_backward * backward_out.reshape(row_count, width)
    )


def solution(mesh):
    in_specs = (
        P(("seg", "head"), None),
        P(("seg", "head"), None),
        P(("seg", "head"), None),
        P("head", None, None),
        P("head", None, None),
        P(None, "head"),
    )
    out_specs = P("seg", "head")
    return jax.shard_map(
        on_device, mesh=mesh, in_specs=in_specs, out_specs=out_specs, check_vma=False
    )
```

profile of v0, /device:TPU:1, one launch (start us, length us, event | category | flops | bytes accessed | tf_op | source)
XLA Modules:
  0.0 661.6 jit_solution(18251715250651719957)
XLA Ops:
  8.2 5.0 all-to-all-start.1
  14.8 3.6 all-to-all-done.1
  18.4 3.4 all-to-all-start.2
  24.9 2.0 all-to-all-done.2
  29.1 2.8 fusion.76
  33.5 2.7 fusion.59
  36.3 3.9 collective-permute-start
  43.0 9.2 %collective-permute-done.1 = bf16[512,384]{1,0:T(8,128)(2,1)S(1)} collective-permute-done((bf16[512,384]{1,0:T(8,128)(2,1)S(1)}, bf16[512,384]{1,0:T(8,128)(2,1)S(1)}, u32[]{:S(2)}, u32[]{:S(2)}) %collective-permute-start.1) | collective-permute-done | bytes 393248 | tf_op jit(solution)/shard_map/ppermute | solution.py:18
  53.2 1.9 collective-permute-start.2
  55.1 11.1 %collective-permute-done.4 = bf16[512,384]{1,0:T(8,128)(2,1)S(1)} collective-permute-done((bf16[512,384]{1,0:T(8,128)(2,1)S(1)}, bf16[512,384]{1,0:T(8,128)(2,1)S(1)}, u32[]{:S(2)}, u32[]{:S(2)}) %collective-permute-start.4) | collective-permute-done | bytes 393248 | tf_op jit(solution)/shard_map/ppermute | solution.py:18
  69.7 3.4 all-to-all-start
  73.1 5.5 all-to-all-done
  80.9 4.2 collective-permute-done.2
  85.0 2.4 pad_maximum_fusion
  87.5 25.0 %collective-permute-done.5 = bf16[1024,384]{1,0:T(8,128)(2,1)} collective-permute-done((bf16[1024,384]{1,0:T(8,128)(2,1)}, bf16[1024,384]{1,0:T(8,128)(2,1)}, u32[]{:S(2)}, u32[]{:S(2)}) %collective-permute-start.5) | collective-permute-done | bytes 786464 | tf_op jit(solution)/shard_map/ppermute | solution.py:18
  112.5 2.4 pad_maximum_fusion.1
  114.9 56.4 %all-gather.7.cloned.1.call-done = f32[384,256,64]{1,2,0:T(8,128)} async-done(((f32[6,256,64]{1,2,0:T(8,128)}), f32[384,256,64]{1,2,0:T(8,128)}) %all-gather.7.cloned.1.call-update) | async-done | bytes 25165840 | tf_op jit(solution)/shard_map/all_gather | solution.py:23
  171.3 116.8 %all-gather.5.cloned.1.call-done = f32[384,64,256]{2,1,0:T(8,128)} async-done(((f32[6,64,256]{2,1,0:T(8,128)}), f32[384,64,256]{2,1,0:T(8,128)}) %all-gather.5.cloned.1.call-update) | async-done | bytes 25165840 | tf_op jit(solution)/shard_map/all_gather | solution.py:23
  288.1 174.3 %while.30 = (s32[]{:T(128)}, f32[6,64,256]{2,1,0:T(8,128)S(1)}, f32[6,256,64]{2,1,0:T(8,128)S(1)}, s32[]{:T(128)}, f32[64,6,64,256]{3,2,1,0:T(8,128)}, /*index=5*/f32[64,6,256,64]{2,3,1,0:T(8,128)}, s32[]{:T(128)}, s32[]{:T(128)}) while((s32[]{:T(128)}, f32[6,64,256]{2,1,0:T(8,128)S(1)}, f32[6,256,64]{2,1,0:T(8,128)S(1)}, ...), condition=%wide.region_9.0_spmd.clone, body=%wide.region_8.0_spmd.clone.sunk | while | flops 589828 | bytes 3932275 | solution.py:35
  466.2 23.6 %while.29 = (s32[]{:T(128)}, f32[256,384]{0,1:T(8,128)S(1)}, bf16[256,384]{1,0:T(8,128)(2,1)S(1)}, bf16[2048,384]{1,0:T(8,128)(2,1)}, bf16[2048,384]{1,0:T(8,128...) while((s32[]{:T(128)}, f32[256,384]{0,1:T(8,128)S(1)}, bf16[256,384]{1,0:T(8,128)(2,1)S(1)}, ...), condition=%wide.region_3.0_spmd, body=%wide.region_0.0_spmd.sunk | while | flops 137887232 | bytes 7478411 | solution.py:68
  476.2 1.8 convolution_dynamic-update-slice_fusion.2
  480.1 1.8 convolution_dynamic-update-slice_fusion.2
  490.1 160.1 %all-reduce.3.cloned.1.call-done = (f32[6,64,256]{2,1,0:T(8,128)}, f32[6,256,64]{1,2,0:T(8,128)}) async-done(((f32[6,64,256]{2,1,0:T(8,128)}, f32[6,256,64]{1,2,0:T(8,128)}), (f32[6,64,256]{2,1,0:T(8,128)}, f32[6,256,64]{1,2,0:T(8,128)})) %all-reduce.3.cloned.1.call-update) | async-done | bytes 786448 | tf_op jit(solution)/shard_map/psum | solution.py:98
  650.2 1.9 fusion.82
  (348 shorter events, 217.8 us)
Async XLA Ops:
  6.5 15.8 %copy-start.1 = (f32[6,64,256]{2,1,0:T(8,128)S(1)}, f32[6,64,256]{2,1,0:T(8,128)}, u32[]{:S(2)}) copy-start(f32[6,64,256]{2,1,0:T(8,128)} %param.13) | copy-start | bytes 1179652
  8.2 10.2 %all-to-all-start.1 = ((bf16[64,4,384]{2,0,1:T(8,128)(2,1)}), bf16[64,4,384]{2,0,1:T(8,128)(2,1)S(1)}, u32[]{:S(2)}, u32[]{:S(2)}) async-start(bf16[64,4,384]{2,0,1:T(8,128)(2,1)} %bitcast.97), calls=%async_computation.1 | async-start | bytes 393216 | tf_op jit(solution)/shard_map/all_to_all | solution.py:78
  18.4 8.5 %all-to-all-start.2 = ((bf16[64,4,384]{2,0,1:T(8,128)(2,1)}), bf16[64,4,384]{2,0,1:T(8,128)(2,1)S(1)}, u32[]{:S(2)}, u32[]{:S(2)}) async-start(bf16[64,4,384]{2,0,1:T(8,128)(2,1)} %bitcast.96), calls=%async_computation.2 | async-start | bytes 393216 | tf_op jit(solution)/shard_map/all_to_all | solution.py:79
  21.8 149.5 %all-gather.7.cloned.1.call-start = ((), (), s32[]{:S(2)}) async-start(), calls=%async_computation.4 | async-start | bytes 25559040 | tf_op jit(solution)/shard_map/all_gather | solution.py:23
  21.8 1.4 copy-start.6
  23.2 1.6 copy-start.3
  27.7 1.4 copy-start.4
  32.0 1.5 copy-start.5
  32.0 256.1 %all-gather.5.cloned.1.call-start = ((), (), s32[]{:S(2)}) async-start(), calls=%async_computation.3 | async-start | bytes 25559040 | tf_op jit(solution)/shard_map/all_gather | solution.py:23
  36.3 5.0 collective-permute-start
  40.2 1.8 collective-permute-start.3
  41.3 10.9 %collective-permute-start.1 = (bf16[512,384]{1,0:T(8,128)(2,1)S(1)}, bf16[512,384]{1,0:T(8,128)(2,1)S(1)}, u32[]{:S(2)}, u32[]{:S(2)}) collective-permute-start(bf16[512,384]{1,0:T(8,128)(2,1)S(1)} %pad_maximum_fusion.4), channel_id=1, source_target_pairs={{0,8},{4,12},{8,0},{12,4},{16,24},{20,28},{24,16},{28,20},{32,40},... | collective-permute-start | bytes 1179656 | tf_op jit(solution)/shard_map/ppermute | solution.py:18
  42.1 26.9 %copy-start.8 = (bf16[64,1536]{1,0:T(8,128)(2,1)S(1)}, bf16[64,1536]{1,0:T(8,128)(2,1)}, u32[]{:S(2)}) copy-start(bf16[64,1536]{1,0:T(8,128)(2,1)} %param.10) | copy-start | bytes 589828
  42.1 24.1 %collective-permute-start.4 = (bf16[512,384]{1,0:T(8,128)(2,1)S(1)}, bf16[512,384]{1,0:T(8,128)(2,1)S(1)}, u32[]{:S(2)}, u32[]{:S(2)}) collective-permute-start(bf16[512,384]{1,0:T(8,128)(2,1)S(1)} %pad_maximum_fusion.5), channel_id=1, source_target_pairs={{0,8},{4,12},{8,0},{12,4},{16,24},{20,28},{24,16},{28,20},{32,40},... | collective-permute-start | bytes 1179656 | tf_op jit(solution)/shard_map/ppermute | solution.py:18
  53.2 19.9 %copy-start.9 = (f32[2,384]{1,0:T(2,128)S(1)}, f32[2,384]{1,0:T(2,128)}, u32[]{:S(2)}) copy-start(f32[2,384]{1,0:T(2,128)} %param.15) | copy-start | bytes 9220
  53.2 31.8 %collective-permute-start.2 = (bf16[1024,384]{1,0:T(8,128)(2,1)}, bf16[1024,384]{1,0:T(8,128)(2,1)}, u32[]{:S(2)}, u32[]{:S(2)}) collective-permute-start(bf16[1024,384]{1,0:T(8,128)(2,1)} %pad_maximum_fusion.2), channel_id=1, source_target_pairs={{0,16},{4,20},{8,24},{12,28},{16,0},{20,4},{24,8},{28,12},{32,48},... | collective-permute-start | bytes 2359304 | tf_op jit(solution)/shard_map/ppermute | solution.py:18
  67.2 45.3 %collective-permute-start.5 = (bf16[1024,384]{1,0:T(8,128)(2,1)}, bf16[1024,384]{1,0:T(8,128)(2,1)}, u32[]{:S(2)}, u32[]{:S(2)}) collective-permute-start(bf16[1024,384]{1,0:T(8,128)(2,1)} %pad_maximum_fusion.3), channel_id=1, source_target_pairs={{0,16},{4,20},{8,24},{12,28},{16,0},{20,4},{24,8},{28,12},{32,48},... | collective-permute-start | bytes 2359304 | tf_op jit(solution)/shard_map/ppermute | solution.py:18
  69.7 8.9 %all-to-all-start = ((bf16[64,4,384]{2,0,1:T(8,128)(2,1)}), bf16[64,4,384]{2,0,1:T(8,128)(2,1)S(1)}, u32[]{:S(2)}, u32[]{:S(2)}) async-start(bf16[64,4,384]{2,0,1:T(8,128)(2,1)} %bitcast.98), calls=%async_computation | async-start | bytes 393216 | tf_op jit(solution)/shard_map/all_to_all | solution.py:77
  288.1 174.6 %copy-start = (f32[6,64,256]{2,1,0:T(8,128)S(1)}, f32[6,64,256]{2,1,0:T(8,128)}, u32[]{:S(2)}) copy-start(f32[6,64,256]{2,1,0:T(8,128)} %fusion.59) | copy-start | bytes 1179652
  462.7 1.0 copy-start.2
  462.7 1.1 copy-start.7
  465.5 184.7 %all-reduce.3.cloned.1.call-start = ((), (), s32[]{:S(2)}) async-start(), calls=%async_computation.5 | async-start | bytes 1572864 | tf_op jit(solution)/shard_map/psum | solution.py:98
  650.2 1.9 copy-start.10
Sparse Core Ops, SparseCore 0:
  32.1 139.1 all-gather.6
  174.0 114.0 all-gather.4
  469.8 180.3 all-reduce.2
where the time goes:
time: 669 us; the launch traced here: 662 us
  waiting for transfers between devices  396 us (59%)
  other arithmetic  100 us (15%)
  local copies, waits for them, and re-layouts  92.1 us (14%)
  matrix products  36.2 us (5%)
  starting transfers between devices  21.2 us (3%)
  between operations  13.5 us (2%)
    all_gather x2, waiting for transfers between devices, entering(): everything = jax.tree.map(lambda part: lax.all_gather(part, axis), shard)  173 us
    psum x1, waiting for transfers between devices, on_device(): total_first, total_second = lax.psum((grad_first, grad_second), 'seg')  160 us
    select_n x128, other arithmetic, lap(): return jax.tree.map(lambda a, b: jnp.where(reached, a, b), new, before)  89.2 us
    dynamic_slice x128, local copies, waits for them, and re-layouts, lap(): new = combine(before, jax.tree.map(lambda part: part[k], everything))  82.4 us
    ppermute x6, waiting for transfers between devices, swapped(): return lax.ppermute(value, axis, pairs)  50.5 us
  transfers between devices with their start and end apart: 12, of which 11 were waited for; matrix products, arithmetic and copies ran while one was open for 6% of the time, Pallas kernels for 0%

commit v1 on v0

v1 whole, which is shorter than its diff:
```python
import jax
import jax.numpy as jnp
from jax import lax
from jax.experimental import pallas as pl
from jax.experimental.pallas import tpu as pltpu
from jax.sharding import PartitionSpec as P

MESH = pl.DeviceIdType.MESH
F32 = jnp.float32
BF16 = jnp.bfloat16

NX, NC, NY, NZ = 4, 2, 4, 8
HEADS = 6
PAIRS = 3
ROWS = 256
WIDTH = 384
HALF = 384
PIECE = HALF // NX
RATE = 0.05
EPS = 1e-5
SCALE = 0.125 * 1.4426950408889634

CHIP_T = BF16
PLANE_T = BF16
BACK_T = F32


def nn(a, b):
    return lax.dot_general(a, b, (((1,), (0,)), ((), ())), preferred_element_type=F32)


def nt(a, b):
    return lax.dot_general(a, b, (((1,), (1,)), ((), ())), preferred_element_type=F32)


def tn(a, b):
    return lax.dot_general(a, b, (((0,), (0,)), ((), ())), preferred_element_type=F32)


def split(x):
    high = x.astype(BF16)
    return high, (x - high.astype(F32)).astype(BF16)


def half_mean(x, ones):
    high, low = split(x)
    return nn(jnp.concatenate([high, low], axis=1), ones)


GELU_A = 0.7978845608028654
GELU_B = 0.044715


def put_weights(dst, index, half, value):
    high, low = split(value)
    dst[index, half * 64 : half * 64 + 64, :] = high
    dst[index, 128 + half * 64 : 128 + half * 64 + 64, :] = low


def kernel(
    q_hbm, k_hbm, v_hbm, w1_hbm, w2_hbm, gate_ref, out_ref,
    ks, vs, qb, w1, w2, w2c, w1s, w2s, act, slope, ones,
    grad, other, chip_out, chips, plane_out, planes, back_out, before, after,
    mine, cross_out, cross, scores, att,
    local_sem, load_sem, a2a_send, a2a_recv, ring_send, ring_recv, core_send, core_recv,
    g_send, g_recv, chip_send, chip_recv, plane_send, plane_recv, back_send, back_recv,
    cross_send, cross_recv,
):
    seg = lax.axis_index("seg")
    y = lax.axis_index("head")
    z = seg // 8
    s = seg % 8
    x = s // 2
    c = s % 2

    def at(zz, xx, cc, yy):
        return {"seg": zz * 8 + xx * 2 + cc, "head": yy}

    def x_peer(d):
        return at(z, (x + d) % NX, c, y)

    twin = at(z, x, 1 - c, y)

    def remote(src, dst, send, recv, device):
        return pltpu.make_async_remote_copy(
            src_ref=src, dst_ref=dst, send_sem=send, recv_sem=recv, device_id=device, device_id_type=MESH
        )

    barrier = pltpu.get_barrier_semaphore()
    peers = [at(z, x, c, (y + d) % NY) for d in range(1, NY)]
    peers += [x_peer(d) for d in range(1, NX)]
    peers += [at((z + d) % NZ, x, c, y) for d in range(1, NZ)]
    peers += [twin]
    for peer in peers:
        pl.semaphore_signal(barrier, inc=1, device_id=peer, device_id_type=MESH)

    load1 = pltpu.make_async_copy(w1_hbm, w1, load_sem.at[0])
    load2 = pltpu.make_async_copy(w2_hbm, w2, load_sem.at[1])
    load1.start()
    load2.start()

    def part(yy):
        return pl.ds(pl.multiple_of(yy * WIDTH, 128), WIDTH)

    rows_of_y = pl.ds(pl.multiple_of(y * 64, 64), 64)
    sources = [k_hbm, v_hbm, q_hbm]
    targets = [ks.at[s, rows_of_y], vs.at[s, rows_of_y], qb.at[rows_of_y]]
    locals_ = []
    for t in range(3):
        copy = pltpu.make_async_copy(sources[t].at[:, part(y)], targets[t], local_sem.at[t])
        copy.start()
        locals_.append(copy)

    pl.semaphore_wait(barrier, len(peers))

    a2a = [[], [], []]
    for t in range(3):
        for d in range(1, NY):
            yy = (y + d) % NY
            copy = remote(
                sources[t].at[:, part(yy)], targets[t], a2a_send.at[t, d], a2a_recv.at[t, d], at(z, x, c, yy)
            )
            copy.start()
            a2a[t].append(copy)

    w1s[...] = jnp.zeros_like(w1s)
    w2s[...] = jnp.zeros_like(w2s)
    row = lax.broadcasted_iota(jnp.int32, (256, 128), 0)
    col = lax.broadcasted_iota(jnp.int32, (256, 128), 1)
    ones[...] = jnp.where((row % 128) // 64 == col // 64, 1.0 / 64, 0.0).astype(BF16)
    load1.wait()
    load2.wait()
    for h in range(HEADS):
        put_weights(w1s, h, h % 2, w1[h])
        flipped = w2[h].T
        flipped = flipped - jnp.mean(flipped, axis=0, keepdims=True)
        w2c[h] = flipped
        put_weights(w2s, h, h % 2, flipped)

    for t in range(2):
        locals_[t].wait()
        for copy in a2a[t]:
            copy.wait()

    kv = (ks, vs)
    first = []
    for t in range(2):
        for j, d in enumerate((1, NX - 1)):
            copy = remote(kv[t].at[s], kv[t].at[s], ring_send.at[t, j], ring_recv.at[t, j], x_peer(d))
            copy.start()
            first.append(copy)
    to_twin = []

    def give(t, slot, k):
        copy = remote(kv[t].at[slot], kv[t].at[slot], core_send.at[t, k], core_recv.at[t, k], twin)
        copy.start()
        to_twin.append(copy)

    for t in range(2):
        give(t, s, 0)

    def grad_pair(p, carry):
        lanes = pl.ds(pl.multiple_of(p * 128, 128), 128)
        keys = ks[s, :, lanes]
        doubled = jnp.concatenate([keys, keys], axis=1)
        centre = jnp.zeros((ROWS, 128), F32)
        for half in range(2):
            h = 2 * p + half
            hidden = nn(doubled, w1s[h])
            square = hidden * hidden
            bent = jnp.tanh(hidden * (GELU_A + GELU_A * GELU_B * square))
            rise = 0.5 + 0.5 * bent
            act[half] = (hidden * rise).astype(BF16)
            slope[half] = rise + 0.5 * hidden * (1.0 - bent * bent) * (GELU_A + 3 * GELU_A * GELU_B * square)
            u = nt(act[half], w2s[h])
            centre = centre + u[:, :128] + u[:, 128:]
        inverse = lax.rsqrt(half_mean(centre * centre, ones[...]) + EPS)
        normal = centre * inverse
        target = vs[s, :, lanes].astype(F32) - keys.astype(F32)
        error = (normal - target) * (1.0 / ROWS)
        du = inverse * (error - half_mean(error, ones[...]) - normal * half_mean(error * normal, ones[...]))
        high, low = split(du)
        both = jnp.concatenate([high, low], axis=1)
        twice = jnp.concatenate([high, high], axis=1)
        for half in range(2):
            h = 2 * p + half
            base = pl.multiple_of(p * 256 + half * 128, 128)
            second = tn(both, act[half])
            second = second[half * 64 : half * 64 + 64] + second[128 + half * 64 : 128 + half * 64 + 64]
            dh = (nn(twice, w2s[h]) * slope[half]).astype(BF16)
            grad[pl.ds(base, 64), :] = tn(keys, dh)[half * 64 : half * 64 + 64]
            grad[pl.ds(base + 64, 64), :] = second
        return carry

    lax.fori_loop(0, PAIRS, grad_pair, 0)

    own_half = pl.ds(pl.multiple_of(c * HALF, HALF), HALF)
    twin_half = pl.ds(pl.multiple_of((1 - c) * HALF, HALF), HALF)
    g_copy = remote(grad.at[twin_half], other, g_send, g_recv, twin)
    g_copy.start()
    g_copy.wait()
    chip_out[...] = (grad[own_half] + other[...]).astype(CHIP_T).reshape(NX, PIECE, 256)
    chip_copies = []
    for d in range(1, NX):
        copy = remote(chip_out.at[(x + d) % NX], chips.at[x], chip_send.at[d], chip_recv.at[d], x_peer(d))
        copy.start()
        chip_copies.append(copy)
    chips[x] = chip_out[x]

    for copy in first:
        copy.wait()
    left, right = (s + 6) % 8, (s + 2) % 8
    second_hop = []
    for t, (slot, d) in enumerate(((left, 1), (right, NX - 1))):
        copy = remote(kv[t].at[slot], kv[t].at[slot], ring_send.at[t, 2], ring_recv.at[t, 2], x_peer(d))
        copy.start()
        second_hop.append(copy)
    for t in range(2):
        give(t, left, 1)
        give(t, right, 2)

    for copy in chip_copies:
        copy.wait()
    plane = chips[0].astype(F32)
    for k in range(1, NX):
        plane = plane + chips[k].astype(F32)
    plane_out[...] = plane.astype(PLANE_T)
    plane_copies = []
    for d in (4, 3, 5, 2, 6, 1, 7):
        copy = remote(plane_out, planes.at[z], plane_send.at[d], plane_recv.at[d], at((z + d) % NZ, x, c, y))
        copy.start()
        plane_copies.append(copy)

    for copy in second_hop:
        copy.wait()
    for t in range(2):
        give(t, (s + 4) % 8, 3)
    locals_[2].wait()
    for copy in a2a[2]:
        copy.wait()
    for copy in to_twin:
        copy.wait()

    lane = lax.broadcasted_iota(jnp.int32, (ROWS, 128), 1)

    def attend(p, carry):
        lanes = pl.ds(pl.multiple_of(p * 128, 128), 128)
        pair = qb[:, lanes]
        result = []
        for half in range(2):
            query = jnp.where(lane // 64 == half, pair, jnp.zeros_like(pair))
            top = None
            for j in range(8):
                block = nt(query, ks[j, :, lanes])
                scores[j] = block
                peak = jnp.maximum(block[:, :128], block[:, 128:])
                top = peak if top is None else jnp.maximum(top, peak)
            top = jnp.max(top, axis=1, keepdims=True)
            total = jnp.zeros((ROWS, 128), F32)
            summed = jnp.zeros((ROWS, 128), F32)
            for j in range(8):
                weight = jnp.exp2((scores[j] - top) * SCALE)
                total = total + weight[:, :128] + weight[:, 128:]
                summed = summed + nn(weight.astype(BF16), vs[j, :, lanes])
            result.append(summed / jnp.sum(total, axis=1, keepdims=True))
        att[:, lanes] = jnp.where(lane < 64, result[0], result[1])
        return carry

    lax.fori_loop(0, 1, attend, 0)

    for copy in plane_copies:
        copy.wait()
    low_sum = jnp.zeros((PIECE, 256), F32)
    high_sum = jnp.zeros((PIECE, 256), F32)
    for d in range(1, NZ):
        zz = (z + d) % NZ
        value = planes[zz].astype(F32)
        low_sum = low_sum + jnp.where(zz < z, value, 0.0)
        high_sum = high_sum + jnp.where(zz > z, value, 0.0)
    ahead_of = []
    run = low_sum
    for k in range(NX):
        ahead_of.append(run)
        run = run + chips[k].astype(F32)
    run = high_sum
    for k in reversed(range(NX)):
        back_out[k, 0] = ahead_of[k].astype(BACK_T)
        back_out[k, 1] = run.astype(BACK_T)
        run = run + chips[k].astype(F32)
    rows_of_x = pl.ds(pl.multiple_of(x * PIECE, PIECE), PIECE)
    back_copies = []
    for d in (2, 1, 3):
        for side, dst in enumerate((before, after)):
            copy = remote(
                back_out.at[(x + d) % NX, side], dst.at[rows_of_x], back_send.at[side, d], back_recv.at[side, d],
                x_peer(d),
            )
            copy.start()
            back_copies.append(copy)
    before[rows_of_x] = back_out[x, 0]
    after[rows_of_x] = back_out[x, 1]

    lax.fori_loop(1, PAIRS, attend, 0)

    for copy in back_copies:
        copy.wait()
    is_one = c.astype(F32)
    is_zero = 1.0 - is_one
    own = grad[own_half]
    oth = other[...]
    cross_out[0] = before[...].astype(F32) + oth + is_zero * own
    cross_out[1] = after[...].astype(F32) + oth + is_one * own
    cross_copies = []
    for side in range(2):
        copy = remote(cross_out.at[side], cross.at[side], cross_send.at[side], cross_recv.at[side], twin)
        copy.start()
        cross_copies.append(copy)
    mine[0] = before[...].astype(F32) + own + is_one * oth
    mine[1] = after[...].astype(F32) + own + is_zero * oth
    for copy in cross_copies:
        copy.wait()
    for side in range(2):
        for h in range(HEADS):
            k = h % 3
            is_own = c if h >= 3 else 1 - c
            sl = slice(k * 128, k * 128 + 64)
            sr = slice(k * 128 + 64, k * 128 + 128)
            keep = is_own > 0
            put_weights(w1s, h, h % 2, w1[h] - RATE * jnp.where(keep, mine[side, sl], cross[side, sl]))
            put_weights(w2s, h, h % 2, w2c[h] - RATE * jnp.where(keep, mine[side, sr], cross[side, sr]))

        def final_pair(p, carry):
            lanes = pl.ds(pl.multiple_of(p * 128, 128), 128)
            query = qb[:, lanes]
            doubled = jnp.concatenate([query, query], axis=1)
            centre = jnp.zeros((ROWS, 128), F32)
            for half in range(2):
                h = 2 * p + half
                hidden = nn(doubled, w1s[h])
                bent = jnp.tanh(hidden * (GELU_A + GELU_A * GELU_B * hidden * hidden))
                high, low = split(hidden * (0.5 + 0.5 * bent))
                u = nt(high, w2s[h])
                centre = centre + u[:, :128] + u[:, 128:] + nt(low, w2s[h, :128, :])
            inverse = lax.rsqrt(half_mean(centre * centre, ones[...]) + EPS)
            gate = jnp.tanh(gate_ref[side : side + 1, lanes])
            att[:, lanes] = att[:, lanes] + gate * (query.astype(F32) + centre * inverse)
            return carry

        lax.fori_loop(0, PAIRS, final_pair, 0)
    out_ref[...] = att[...]


def on_device(queries, key_rows, value_rows, w_first, w_second, gate_pairs):
    dma = pltpu.SemaphoreType.DMA
    hbm = pl.BlockSpec(memory_space=pl.ANY)
    vmem = pl.BlockSpec(memory_space=pltpu.VMEM)
    scratch = [
        pltpu.VMEM((8, ROWS, WIDTH), BF16),
        pltpu.VMEM((8, ROWS, WIDTH), BF16),
        pltpu.VMEM((ROWS, WIDTH), BF16),
        pltpu.VMEM((HEADS, 64, 256), F32),
        pltpu.VMEM((HEADS, 256, 64), F32),
        pltpu.VMEM((HEADS, 64, 256), F32),
        pltpu.VMEM((HEADS, 256, 256), BF16),
        pltpu.VMEM((HEADS, 256, 256), BF16),
        pltpu.VMEM((2, ROWS, 256), BF16),
        pltpu.VMEM((2, ROWS, 256), F32),
        pltpu.VMEM((256, 128), BF16),
        pltpu.VMEM((2 * HALF, 256), F32),
        pltpu.VMEM((HALF, 256), F32),
        pltpu.VMEM((NX, PIECE, 256), CHIP_T),
        pltpu.VMEM((NX, PIECE, 256), CHIP_T),
        pltpu.VMEM((PIECE, 256), PLANE_T),
        pltpu.VMEM((NZ, PIECE, 256), PLANE_T),
        pltpu.VMEM((NX, 2, PIECE, 256), BACK_T),
        pltpu.VMEM((HALF, 256), BACK_T),
        pltpu.VMEM((HALF, 256), BACK_T),
        pltpu.VMEM((2, HALF, 256), F32),
        pltpu.VMEM((2, HALF, 256), F32),
        pltpu.VMEM((2, HALF, 256), F32),
        pltpu.VMEM((8, ROWS, 256), F32),
        pltpu.VMEM((ROWS, WIDTH), F32),
        dma((3,)),
        dma((2,)),
        dma((3, NY)),
        dma((3, NY)),
        dma((2, 3)),
        dma((2, 3)),
        dma((2, 4)),
        dma((2, 4)),
        dma,
        dma,
        dma((NX,)),
        dma((NX,)),
        dma((NZ,)),
        dma((NZ,)),
        dma((2, NX)),
        dma((2, NX)),
        dma((2,)),
        dma((2,)),
    ]
    return pl.pallas_call(
        kernel,
        out_shape=jax.ShapeDtypeStruct((ROWS, WIDTH), F32),
        in_specs=[hbm, hbm, hbm, hbm, hbm, vmem],
        out_specs=vmem,
        scratch_shapes=scratch,
        compiler_params=pltpu.CompilerParams(
            collective_id=0, has_side_effects=True, vmem_limit_bytes=48 * 1024 * 1024
        ),
        name="layer",
    )(queries, key_rows, value_rows, w_first, w_second, gate_pairs)


def solution(mesh):
    in_specs = (
        P(("seg", "head"), None),
        P(("seg", "head"), None),
        P(("seg", "head"), None),
        P("head", None, None),
        P("head", None, None),
        P(None, "head"),
    )
    out_specs = P("seg", "head")
    return jax.shard_map(on_device, mesh=mesh, in_specs=in_specs, out_specs=out_specs, check_vma=False)
```

time: 669 us -> 58.5 us (0.09); the launches traced: 662 us -> 58.4 us
  waiting for transfers between devices: 396 us -> 0 us
  other arithmetic: 100 us -> 0 us
  local copies, waits for them, and re-layouts: 92.1 us -> 2.11 us
  Pallas kernels: 0 us -> 56.2 us
  matrix products: 36.2 us -> 0 us
  starting transfers between devices: 21.2 us -> 0 us
  between operations: 13.5 us -> 0.08 us
    all_gather x2 -> x0, waiting for transfers between devices: 173 us -> none  [entering(): everything = jax.tree.map(lambda part: lax.all_gather(part, axis), shard)]
    psum x1 -> x0, waiting for transfers between devices: 160 us -> none  [on_device(): total_first, total_second = lax.psum((grad_first, grad_second), 'seg')]
    select_n x128 -> x0, other arithmetic: 89.2 us -> none  [lap(): return jax.tree.map(lambda a, b: jnp.where(reached, a, b), new, before)]
    dynamic_slice x128 -> x0, local copies, waits for them, and re-layouts: 82.4 us -> none  [lap(): new = combine(before, jax.tree.map(lambda part: part[k], everything))]
    pallas_call x0 -> x1, Pallas kernels: none -> 56.2 us  [on_device(): pl.pallas_call(kernel, out_shape=jax.ShapeDtypeStruct((ROWS, WIDTH), F32)...]
    ppermute x6 -> x0, waiting for transfers between devices: 50.5 us -> none  [swapped(): return lax.ppermute(value, axis, pairs)]
    dot_general x21 -> x0, matrix products: 36.2 us -> none  [the longest x6 10.9 us: head_step(): attended = jnp.dot(weights, head_value, preferred_element_type=jnp.float32)]
    all_to_all x3 -> x0, starting transfers between devices: 11.7 us -> none  [the longest x1 5 us: on_device(): lax.all_to_all(key_rows, 'head', split_axis=1, concat_axis=0, tiled=True)]
  transfers between devices with their start and end apart: 12 -> 0, of which waited for: 11 -> 0; matrix products, arithmetic and copies ran while one was open for 6% -> 0% of each run, Pallas kernels for 0% -> 0%
where the time goes in v1:
time: 58.5 us; the launch traced here: 58.4 us
  Pallas kernels  56.2 us (96%)
  local copies, waits for them, and re-layouts  2.11 us (4%)
    pallas_call x1, Pallas kernels, on_device(): pl.pallas_call(kernel, out_shape=jax.ShapeDtypeStruct((ROWS, WIDTH), F32)...  56.2 us
    unnamed x12, local copies, waits for them, and re-layouts  2.11 us

profile of v1, /device:TPU:1, one launch (start us, length us, event | category | flops | bytes accessed | tf_op | source)
XLA Modules:
  0.0 58.4 jit_solution(2735016619153156349)
XLA Ops:
  0.0 0.0 copy-start.4
  0.0 0.0 copy-start
  0.0 0.0 copy-start.3
  0.0 0.0 copy-start.2
  0.0 0.0 copy-start.1
  0.0 1.3 %copy.7.w2_hbm = f32[6,256,64]{2,1,0:T(8,128)S(1)} copy(f32[6,256,64]{1,2,0:T(8,128)} %param.10) | data formatting | bytes 786432 | tf_op args[4]
  1.4 0.0 copy-done.4
  1.4 0.0 copy-done
  1.4 0.0 copy-done.3
  1.4 0.0 copy-done.2
  1.4 0.0 copy-done.1
  1.4 56.2 %layer.1 = f32[256,384]{1,0:T(8,128)S(1)} custom-call(bf16[64,1536]{1,0:T(8,128)(2,1)S(1)} %copy-done.1, bf16[64,1536]{1,0:T(8,128)(2,1)S(1)} %copy-done.2, bf16[64,1536]{1,0:T(8,128)(2,1)S(1)} %copy-done.3, f32[6,64,256]{2,1,0:T(8,128)S(1)} %copy-done, f32[6,256,64]{2,1,0:T(8,128)S(1)} %copy.7.w2_hbm, f32[2,384]{1,0:T(2,128)S(1)} %copy-done.4), custom_call_target="tpu_custom_call" | custom-call | tf_op jit(solution)/shard_map/layer/pallas_call | solution.py:402
  57.6 0.7 %copy.9 = f32[256,384]{1,0:T(8,128)} copy(f32[256,384]{1,0:T(8,128)S(1)} %layer.1) | data formatting | bytes 786432
Async XLA Ops:
  0.0 1.4 %copy-start.4 = (f32[2,384]{1,0:T(2,128)S(1)}, f32[2,384]{1,0:T(2,128)}, u32[]{:S(2)}) copy-start(f32[2,384]{1,0:T(2,128)} %gate_ref.1) | copy-start | bytes 9220
  0.0 1.4 %copy-start = (f32[6,64,256]{2,1,0:T(8,128)S(1)}, f32[6,64,256]{2,1,0:T(8,128)}, u32[]{:S(2)}) copy-start(f32[6,64,256]{2,1,0:T(8,128)} %w1_hbm.1) | copy-start | bytes 1179652
  0.0 1.4 %copy-start.3 = (bf16[64,1536]{1,0:T(8,128)(2,1)S(1)}, bf16[64,1536]{1,0:T(8,128)(2,1)}, u32[]{:S(2)}) copy-start(bf16[64,1536]{1,0:T(8,128)(2,1)} %v_hbm.1) | copy-start | bytes 589828
  0.0 1.4 %copy-start.2 = (bf16[64,1536]{1,0:T(8,128)(2,1)S(1)}, bf16[64,1536]{1,0:T(8,128)(2,1)}, u32[]{:S(2)}) copy-start(bf16[64,1536]{1,0:T(8,128)(2,1)} %k_hbm.1) | copy-start | bytes 589828
  0.0 1.4 %copy-start.1 = (bf16[64,1536]{1,0:T(8,128)(2,1)S(1)}, bf16[64,1536]{1,0:T(8,128)(2,1)}, u32[]{:S(2)}) copy-start(bf16[64,1536]{1,0:T(8,128)(2,1)} %q_hbm.1) | copy-start | bytes 589828

commit v2 on v0

v2 whole, which is shorter than its diff:
```python
import jax
import jax.numpy as jnp
from jax import lax
from jax.experimental import pallas as pl
from jax.experimental.pallas import tpu as pltpu
from jax.sharding import PartitionSpec as P

MESH = pl.DeviceIdType.MESH
F32 = jnp.float32
BF16 = jnp.bfloat16

NX, NC, NY, NZ = 4, 2, 4, 8
HEADS = 6
PAIRS = 3
ROWS = 256
WIDTH = 384
BLOCK = 128
PIECE = BLOCK // NX
RATE = 0.05
EPS = 1e-5
SCALE = 0.125 * 1.4426950408889634

CHIP_T = BF16
PLANE_T = BF16
BACK_T = F32


def nn(a, b):
    return lax.dot_general(a, b, (((1,), (0,)), ((), ())), preferred_element_type=F32)


def nt(a, b):
    return lax.dot_general(a, b, (((1,), (1,)), ((), ())), preferred_element_type=F32)


def tn(a, b):
    return lax.dot_general(a, b, (((0,), (0,)), ((), ())), preferred_element_type=F32)


def split(x):
    high = x.astype(BF16)
    return high, (x - high.astype(F32)).astype(BF16)


def half_mean(x, ones):
    high, low = split(x)
    return nn(jnp.concatenate([high, low], axis=1), ones)


GELU_A = 0.7978845608028654
GELU_B = 0.044715


def put_weights(dst, rows, value):
    high, low = split(value)
    dst[pl.ds(rows, 64), :] = high
    dst[pl.ds(rows + 128, 64), :] = low


def kernel(
    q_hbm, k_hbm, v_hbm, w1_hbm, w2_hbm, gate_ref, out_ref,
    kv, qb, w1, w2, w2c, w1s, w2s, act, slope, ones,
    grad, other, chip_out, chips, plane_out, planes, back_out, back,
    cross_out, cross, centres, scores, att,
    local_sem, load_sem, a2a_send, a2a_recv, q_send, q_recv, ring_send, ring_recv, core_send, core_recv,
    g_send, g_recv, chip_send, chip_recv, plane_send, plane_recv, back_send, back_recv,
    cross_send, cross_recv,
):
    seg = lax.axis_index("seg")
    y = lax.axis_index("head")
    z = seg // 8
    s = seg % 8
    x = s // 2
    c = s % 2

    def at(zz, xx, cc, yy):
        return {"seg": zz * 8 + xx * 2 + cc, "head": yy}

    def x_peer(d):
        return at(z, (x + d) % NX, c, y)

    twin = at(z, x, 1 - c, y)

    def send(src, dst, send_sem, recv_sem, device):
        copy = pltpu.make_async_remote_copy(
            src_ref=src, dst_ref=dst, send_sem=send_sem, recv_sem=recv_sem, device_id=device, device_id_type=MESH
        )
        copy.start()
        return copy

    def wait(copies):
        for copy in copies:
            copy.wait()

    barrier = pltpu.get_barrier_semaphore()
    peers = [at((z + d) % NZ, x, c, y) for d in range(1, NZ)]
    peers += [at(z, x, c, (y + d) % NY) for d in range(1, NY)]
    peers += [x_peer(d) for d in range(1, NX)]
    peers += [twin]
    for peer in peers:
        pl.semaphore_signal(barrier, inc=1, device_id=peer, device_id_type=MESH)

    load1 = pltpu.make_async_copy(w1_hbm, w1, load_sem.at[0])
    load2 = pltpu.make_async_copy(w2_hbm, w2, load_sem.at[1])
    load1.start()
    load2.start()

    def part(yy, p):
        return pl.ds(pl.multiple_of(yy * WIDTH + p * 128, 128), 128)

    rows_of_y = pl.ds(pl.multiple_of(y * 64, 64), 64)
    sources = (k_hbm, v_hbm)
    own_tokens = [[], [], []]
    for p in range(PAIRS):
        for t in range(2):
            copy = pltpu.make_async_copy(
                sources[t].at[:, part(y, p)], kv.at[p, s, t, rows_of_y], local_sem.at[p, t]
            )
            copy.start()
            own_tokens[p].append(copy)
    own_query = []
    for p in range(PAIRS):
        copy = pltpu.make_async_copy(q_hbm.at[:, part(y, p)], qb.at[p, rows_of_y], local_sem.at[p, 2])
        copy.start()
        own_query.append(copy)

    w1s[...] = jnp.zeros_like(w1s)
    w2s[...] = jnp.zeros_like(w2s)
    row = lax.broadcasted_iota(jnp.int32, (256, 128), 0)
    col = lax.broadcasted_iota(jnp.int32, (256, 128), 1)
    ones[...] = jnp.where((row % 128) // 64 == col // 64, 1.0 / 64, 0.0).astype(BF16)
    load1.wait()
    load2.wait()
    for h in range(HEADS):
        put_weights(w1s.at[0, h], h % 2 * 64, w1[h])
        centred = w2[h] - jnp.mean(w2[h], axis=0, keepdims=True)
        w2c[h] = centred
        put_weights(w2s.at[0, h], h % 2 * 64, centred)

    pl.semaphore_wait(barrier, len(peers))

    tokens = [[], [], []]
    for p in range(PAIRS):
        for d in (2, 1, 3):
            yy = (y + d) % NY
            for t in range(2):
                tokens[p].append(
                    send(
                        sources[t].at[:, part(yy, p)], kv.at[p, s, t, rows_of_y],
                        a2a_send.at[p, t, d], a2a_recv.at[p, t, d], at(z, x, c, yy),
                    )
                )
    query_copies = []
    for p in range(PAIRS):
        for d in (2, 1, 3):
            yy = (y + d) % NY
            query_copies.append(
                send(
                    q_hbm.at[:, part(yy, p)], qb.at[p, rows_of_y], q_send.at[p, d], q_recv.at[p, d],
                    at(z, x, c, yy),
                )
            )

    def gradients(p):
        keys = kv[p, s, 0]
        doubled = jnp.concatenate([keys, keys], axis=1)
        centre = jnp.zeros((ROWS, 128), F32)
        for half in range(2):
            h = 2 * p + half
            hidden = nn(doubled, w1s[0, h])
            square = hidden * hidden
            bent = jnp.tanh(hidden * (GELU_A + GELU_A * GELU_B * square))
            rise = 0.5 + 0.5 * bent
            act[half] = (hidden * rise).astype(BF16)
            slope[half] = rise + 0.5 * hidden * (1.0 - bent * bent) * (GELU_A + 3 * GELU_A * GELU_B * square)
            u = nt(act[half], w2s[0, h])
            centre = centre + u[:, :128] + u[:, 128:]
        inverse = lax.rsqrt(half_mean(centre * centre, ones[...]) + EPS)
        normal = centre * inverse
        target = kv[p, s, 1].astype(F32) - keys.astype(F32)
        error = (normal - target) * (1.0 / ROWS)
        du = inverse * (error - half_mean(error, ones[...]) - normal * half_mean(error * normal, ones[...]))
        high, low = split(du)
        both = jnp.concatenate([high, low], axis=1)
        twice = jnp.concatenate([high, high], axis=1)
        for half in range(2):
            second = tn(both, act[half])
            second = second[half * 64 : half * 64 + 64] + second[128 + half * 64 : 128 + half * 64 + 64]
            dh = (nn(twice, w2s[0, 2 * p + half]) * slope[half]).astype(BF16)
            grad[p, half, :64] = tn(keys, dh)[half * 64 : half * 64 + 64]
            grad[p, half, 64:] = second

    def to_other_core(p):
        return send(grad.at[p, 1 - c], other.at[p], g_send.at[p], g_recv.at[p], twin)

    def along_x(p):
        chip_out[p] = (grad[p, c] + other[p]).astype(CHIP_T).reshape(NX, PIECE, 256)
        copies = [
            send(chip_out.at[p, (x + d) % NX], chips.at[p, x], chip_send.at[p, d], chip_recv.at[p, d], x_peer(d))
            for d in (2, 1, 3)
        ]
        chips[p, x] = chip_out[p, x]
        return copies

    def along_z(p):
        plane = chips[p, 0].astype(F32)
        for k in range(1, NX):
            plane = plane + chips[p, k].astype(F32)
        plane_out[p] = plane.astype(PLANE_T)
        return [
            send(
                plane_out.at[p], planes.at[p, z], plane_send.at[p, d], plane_recv.at[p, d],
                at((z + d) % NZ, x, c, y),
            )
            for d in (4, 3, 5, 2, 6, 1, 7)
        ]

    def back_along_x(p):
        low_sum = jnp.zeros((PIECE, 256), F32)
        high_sum = jnp.zeros((PIECE, 256), F32)
        for d in range(1, NZ):
            zz = (z + d) % NZ
            value = planes[p, zz].astype(F32)
            low_sum = low_sum + jnp.where(zz < z, value, 0.0)
            high_sum = high_sum + jnp.where(zz > z, value, 0.0)
        ahead_of = []
        run = low_sum
        for k in range(NX):
            ahead_of.append(run)
            run = run + chips[p, k].astype(F32)
        run = high_sum
        for k in reversed(range(NX)):
            back_out[p, k, 0] = ahead_of[k].astype(BACK_T)
            back_out[p, k, 1] = run.astype(BACK_T)
            run = run + chips[p, k].astype(F32)
        copies = [
            send(back_out.at[p, (x + d) % NX], back.at[p, x], back_send.at[p, d], back_recv.at[p, d], x_peer(d))
            for d in (2, 1, 3)
        ]
        back[p, x] = back_out[p, x]
        return copies

    is_one = c.astype(F32)
    is_zero = 1.0 - is_one

    def to_twin(p):
        own, oth = grad[p, c], other[p]
        ahead = back[p, :, 0].reshape(BLOCK, 256).astype(F32) + oth
        behind = back[p, :, 1].reshape(BLOCK, 256).astype(F32) + oth
        cross_out[p, 0] = ahead + is_zero * own
        cross_out[p, 1] = behind + is_one * own
        return [send(cross_out.at[p], cross.at[p], cross_send.at[p], cross_recv.at[p], twin)]

    def inner(p, half, side, value):
        h = 2 * p + half
        rows = pl.multiple_of(half * 64, 64)
        put_weights(w1s.at[side, h], rows, w1[h] - RATE * value[:64])
        put_weights(w2s.at[side, h], rows, w2c[h] - RATE * value[64:])
        query = qb[p]
        hidden = nn(jnp.concatenate([query, query], axis=1), w1s[side, h])
        bent = jnp.tanh(hidden * (GELU_A + GELU_A * GELU_B * hidden * hidden))
        high, low = split(hidden * (0.5 + 0.5 * bent))
        u = nt(high, w2s[side, h])
        return u[:, :128] + u[:, 128:] + nt(low, w2s[side, h, :128, :])

    def own_inner(p):
        own, oth = grad[p, c], other[p]
        ahead = back[p, :, 0].reshape(BLOCK, 256).astype(F32) + own + is_one * oth
        behind = back[p, :, 1].reshape(BLOCK, 256).astype(F32) + own + is_zero * oth
        centres[p, 0] = inner(p, c, 0, ahead)
        centres[p, 1] = inner(p, c, 1, behind)

    def finish(p):
        query = qb[p].astype(F32)
        result = att[p]
        for side in range(2):
            centre = centres[p, side] + inner(p, 1 - c, side, cross[p, side])
            inverse = lax.rsqrt(half_mean(centre * centre, ones[...]) + EPS)
            gate = jnp.tanh(gate_ref[side : side + 1, p * 128 : p * 128 + 128])
            result = result + gate * (query + centre * inverse)
        out_ref[:, p * 128 : p * 128 + 128] = result

    left, right, far = (s + 6) % 8, (s + 2) % 8, (s + 4) % 8
    given = [[], [], []]

    def give(p, slot, k):
        given[p].append(send(kv.at[p, slot], kv.at[p, slot], core_send.at[p, k], core_recv.at[p, k], twin))

    def first_hop(p):
        give(p, s, 0)
        return [
            send(kv.at[p, s], kv.at[p, s], ring_send.at[p, k], ring_recv.at[p, k], x_peer(d))
            for k, d in enumerate((1, NX - 1))
        ]

    def second_hop(p):
        copies = [
            send(kv.at[p, slot, t], kv.at[p, slot, t], ring_send.at[p, 2 + t], ring_recv.at[p, 2 + t], x_peer(d))
            for t, (slot, d) in enumerate(((left, 1), (right, NX - 1)))
        ]
        give(p, left, 1)
        give(p, right, 2)
        return copies

    lane = lax.broadcasted_iota(jnp.int32, (ROWS, 128), 1)

    def attend(p):
        pair = qb[p]

        def one(half):
            query = jnp.where(lane // 64 == half, pair, jnp.zeros_like(pair))
            top = None
            for j in range(8):
                block = nt(query, kv[p, j, 0])
                scores[j] = block
                peak = jnp.maximum(block[:, :128], block[:, 128:])
                top = peak if top is None else jnp.maximum(top, peak)
            top = jnp.max(top, axis=1, keepdims=True)
            total = jnp.zeros((ROWS, 128), F32)
            summed = jnp.zeros((ROWS, 128), F32)
            for j in range(8):
                weight = jnp.exp2((scores[j] - top) * SCALE)
                total = total + weight[:, :128] + weight[:, 128:]
                summed = summed + nn(weight.astype(BF16), kv[p, j, 1])
            return summed / jnp.sum(total, axis=1, keepdims=True)

        first = one(0)
        att[p] = jnp.where(lane < 64, first, one(1))

    wait(own_tokens[0] + tokens[0])
    hop0 = first_hop(0)
    gradients(0)
    swap0 = to_other_core(0)
    wait(own_tokens[1] + tokens[1])
    gradients(1)
    swap1 = to_other_core(1)
    swap0.wait()
    chip0 = along_x(0)
    hop1 = first_hop(1)
    wait(own_tokens[2] + tokens[2])
    gradients(2)
    swap2 = to_other_core(2)
    swap1.wait()
    chip1 = along_x(1)
    wait(chip0)
    plane0 = along_z(0)
    swap2.wait()
    chip2 = along_x(2)
    hop2 = first_hop(2)
    wait(hop0)
    more0 = second_hop(0)
    wait(chip1)
    plane1 = along_z(1)
    wait(chip2)
    plane2 = along_z(2)
    wait(hop1)
    more1 = second_hop(1)
    wait(more0)
    give(0, far, 3)
    wait(own_query + query_copies)
    wait(given[0])
    attend(0)
    wait(hop2)
    more2 = second_hop(2)
    wait(plane0)
    back0 = back_along_x(0)
    wait(more1)
    give(1, far, 3)
    wait(plane1)
    back1 = back_along_x(1)
    wait(given[1])
    attend(1)
    wait(plane2)
    back2 = back_along_x(2)
    wait(more2)
    give(2, far, 3)
    wait(back0)
    cross0 = to_twin(0)
    own_inner(0)
    wait(given[2])
    attend(2)
    wait(back1)
    cross1 = to_twin(1)
    own_inner(1)
    wait(cross0)
    finish(0)
    wait(back2)
    cross2 = to_twin(2)
    own_inner(2)
    wait(cross1)
    finish(1)
    wait(cross2)
    finish(2)


def on_device(queries, key_rows, value_rows, w_first, w_second, gate_pairs):
    dma = pltpu.SemaphoreType.DMA
    hbm = pl.BlockSpec(memory_space=pl.ANY)
    vmem = pl.BlockSpec(memory_space=pltpu.VMEM)
    scratch = [
        pltpu.VMEM((PAIRS, 8, 2, ROWS, 128), BF16),
        pltpu.VMEM((PAIRS, ROWS, 128), BF16),
        pltpu.VMEM((HEADS, 64, 256), F32),
        pltpu.VMEM((HEADS, 64, 256), F32),
        pltpu.VMEM((HEADS, 64, 256), F32),
        pltpu.VMEM((2, HEADS, 256, 256), BF16),
        pltpu.VMEM((2, HEADS, 256, 256), BF16),
        pltpu.VMEM((2, ROWS, 256), BF16),
        pltpu.VMEM((2, ROWS, 256), F32),
        pltpu.VMEM((256, 128), BF16),
        pltpu.VMEM((PAIRS, 2, BLOCK, 256), F32),
        pltpu.VMEM((PAIRS, BLOCK, 256), F32),
        pltpu.VMEM((PAIRS, NX, PIECE, 256), CHIP_T),
        pltpu.VMEM((PAIRS, NX, PIECE, 256), CHIP_T),
        pltpu.VMEM((PAIRS, PIECE, 256), PLANE_T),
        pltpu.VMEM((PAIRS, NZ, PIECE, 256), PLANE_T),
        pltpu.VMEM((PAIRS, NX, 2, PIECE, 256), BACK_T),
        pltpu.VMEM((PAIRS, NX, 2, PIECE, 256), BACK_T),
        pltpu.VMEM((PAIRS, 2, BLOCK, 256), F32),
        pltpu.VMEM((PAIRS, 2, BLOCK, 256), F32),
        pltpu.VMEM((PAIRS, 2, ROWS, 128), F32),
        pltpu.VMEM((8, ROWS, 256), F32),
        pltpu.VMEM((PAIRS, ROWS, 128), F32),
        dma((PAIRS, 3)),
        dma((2,)),
        dma((PAIRS, 2, NY)),
        dma((PAIRS, 2, NY)),
        dma((PAIRS, NY)),
        dma((PAIRS, NY)),
        dma((PAIRS, 4)),
        dma((PAIRS, 4)),
        dma((PAIRS, 4)),
        dma((PAIRS, 4)),
        dma((PAIRS,)),
        dma((PAIRS,)),
        dma((PAIRS, NX)),
        dma((PAIRS, NX)),
        dma((PAIRS, NZ)),
        dma((PAIRS, NZ)),
        dma((PAIRS, NX)),
        dma((PAIRS, NX)),
        dma((PAIRS,)),
        dma((PAIRS,)),
    ]
    return pl.pallas_call(
        kernel,
        out_shape=jax.ShapeDtypeStruct((ROWS, WIDTH), F32),
        in_specs=[hbm, hbm, hbm, hbm, hbm, vmem],
        out_specs=vmem,
        scratch_shapes=scratch,
        compiler_params=pltpu.CompilerParams(
            collective_id=0, has_side_effects=True, vmem_limit_bytes=62 * 1024 * 1024
        ),
        name="layer",
    )(queries, key_rows, value_rows, w_first, jnp.swapaxes(w_second, 1, 2), gate_pairs)


def solution(mesh):
    in_specs = (
        P(("seg", "head"), None),
        P(("seg", "head"), None),
        P(("seg", "head"), None),
        P("head", None, None),
        P("head", None, None),
        P(None, "head"),
    )
    out_specs = P("seg", "head")
    return jax.shard_map(on_device, mesh=mesh, in_specs=in_specs, out_specs=out_specs, check_vma=False)
```

time: 669 us -> 52.9 us (0.08); the launches traced: 662 us -> 52.7 us
  waiting for transfers between devices: 396 us -> 0 us
  other arithmetic: 100 us -> 0 us
  local copies, waits for them, and re-layouts: 92.1 us -> 1.77 us
  Pallas kernels: 0 us -> 51 us
  matrix products: 36.2 us -> 0 us
  starting transfers between devices: 21.2 us -> 0 us
  between operations: 13.5 us -> 0.01 us
    all_gather x2 -> x0, waiting for transfers between devices: 173 us -> none  [entering(): everything = jax.tree.map(lambda part: lax.all_gather(part, axis), shard)]
    psum x1 -> x0, waiting for transfers between devices: 160 us -> none  [on_device(): total_first, total_second = lax.psum((grad_first, grad_second), 'seg')]
    select_n x128 -> x0, other arithmetic: 89.2 us -> none  [lap(): return jax.tree.map(lambda a, b: jnp.where(reached, a, b), new, before)]
    dynamic_slice x128 -> x0, local copies, waits for them, and re-layouts: 82.4 us -> none  [lap(): new = combine(before, jax.tree.map(lambda part: part[k], everything))]
    pallas_call x0 -> x1, Pallas kernels: none -> 51 us  [on_device(): pl.pallas_call(kernel, out_shape=jax.ShapeDtypeStruct((ROWS, WIDTH), F32)...]
    ppermute x6 -> x0, waiting for transfers between devices: 50.5 us -> none  [swapped(): return lax.ppermute(value, axis, pairs)]
    dot_general x21 -> x0, matrix products: 36.2 us -> none  [the longest x6 10.9 us: head_step(): attended = jnp.dot(weights, head_value, preferred_element_type=jnp.float32)]
    all_to_all x3 -> x0, starting transfers between devices: 11.7 us -> none  [the longest x1 5 us: on_device(): lax.all_to_all(key_rows, 'head', split_axis=1, concat_axis=0, tiled=True)]
  transfers between devices with their start and end apart: 12 -> 0, of which waited for: 11 -> 0; matrix products, arithmetic and copies ran while one was open for 6% -> 0% of each run, Pallas kernels for 0% -> 0%
where the time goes in v2:
time: 52.9 us; the launch traced here: 52.7 us
  Pallas kernels  51 us (96%)
  local copies, waits for them, and re-layouts  1.77 us (3%)
    pallas_call x1, Pallas kernels, on_device(): pl.pallas_call(kernel, out_shape=jax.ShapeDtypeStruct((ROWS, WIDTH), F32)...  51 us
    unnamed x1, local copies, waits for them, and re-layouts  1.77 us

profile of v2, /device:TPU:1, one launch (start us, length us, event | category | flops | bytes accessed | tf_op | source)
XLA Modules:
  0.0 52.7 jit_solution(9207325649044651163)
XLA Ops:
  0.0 51.0 %layer.1 = f32[256,384]{1,0:T(8,128)} custom-call(bf16[64,1536]{1,0:T(8,128)(2,1)} %q_hbm.1, bf16[64,1536]{1,0:T(8,128)(2,1)} %k_hbm.1, bf16[64,1536]{1,0:T(8,128)(2,1)} %v_hbm.1, f32[6,64,256]{2,1,0:T(8,128)} %w1_hbm.1, f32[6,64,256]{2,1,0:T(8,128)} %bitcast.1, f32[2,384]{1,0:T(2,128)} %gate_ref.1), custom_call_target="tpu_custom_call" | custom-call | tf_op jit(solution)/shard_map/layer/pallas_call | solution.py:445
  51.0 1.8 %copy.8 = f32[256,384]{1,0:T(8,128)} copy(f32[256,384]{1,0:T(8,128)} %layer.1) | data formatting | bytes 786432

commit v3 on v2

--- a/solution.py
+++ b/solution.py
@@ -22,7 +22,6 @@
 
 CHIP_T = BF16
 PLANE_T = BF16
-BACK_T = F32
 
 
 def nn(a, b):
@@ -60,8 +59,8 @@
 def kernel(
     q_hbm, k_hbm, v_hbm, w1_hbm, w2_hbm, gate_ref, out_ref,
     kv, qb, w1, w2, w2c, w1s, w2s, act, slope, ones,
-    grad, other, chip_out, chips, plane_out, planes, back_out, back,
-    cross_out, cross, centres, scores, att,
+    grad, other, chip_out, chips, plane_out, planes, part_out, part_in, total_out, total_in,
+    cross_out, cross, centres, scores, att, tops, totals, sums,
     local_sem, load_sem, a2a_send, a2a_recv, q_send, q_recv, ring_send, ring_recv, core_send, core_recv,
     g_send, g_recv, chip_send, chip_recv, plane_send, plane_recv, back_send, back_recv,
     cross_send, cross_recv,
@@ -215,6 +214,8 @@
             for d in (4, 3, 5, 2, 6, 1, 7)
         ]
 
+    low_plane = z < NZ // 2
+
     def back_along_x(p):
         low_sum = jnp.zeros((PIECE, 256), F32)
         high_sum = jnp.zeros((PIECE, 256), F32)
@@ -228,27 +229,37 @@
         for k in range(NX):
             ahead_of.append(run)
             run = run + chips[p, k].astype(F32)
+        total_out[p] = run + high_sum
         run = high_sum
         for k in reversed(range(NX)):
-            back_out[p, k, 0] = ahead_of[k].astype(BACK_T)
-            back_out[p, k, 1] = run.astype(BACK_T)
+            part_out[p, k] = jnp.where(low_plane, ahead_of[k], run).astype(BF16)
             run = run + chips[p, k].astype(F32)
-        copies = [
-            send(back_out.at[p, (x + d) % NX], back.at[p, x], back_send.at[p, d], back_recv.at[p, d], x_peer(d))
-            for d in (2, 1, 3)
-        ]
-        back[p, x] = back_out[p, x]
+        copies = []
+        for d in (2, 1, 3):
+            to = x_peer(d)
+            copies.append(
+                send(part_out.at[p, (x + d) % NX], part_in.at[p, x], back_send.at[p, 0, d], back_recv.at[p, 0, d], to)
+            )
+            copies.append(
+                send(total_out.at[p], total_in.at[p, x], back_send.at[p, 1, d], back_recv.at[p, 1, d], to)
+            )
+        part_in[p, x] = part_out[p, x]
+        total_in[p, x] = total_out[p]
         return copies
 
     is_one = c.astype(F32)
     is_zero = 1.0 - is_one
 
+    def around(p):
+        near = part_in[p].reshape(BLOCK, 256).astype(F32)
+        rest = total_in[p].reshape(BLOCK, 256) - chip_out[p].reshape(BLOCK, 256).astype(F32) - near
+        return jnp.where(low_plane, near, rest), jnp.where(low_plane, rest, near)
+
     def to_twin(p):
         own, oth = grad[p, c], other[p]
-        ahead = back[p, :, 0].reshape(BLOCK, 256).astype(F32) + oth
-        behind = back[p, :, 1].reshape(BLOCK, 256).astype(F32) + oth
-        cross_out[p, 0] = ahead + is_zero * own
-        cross_out[p, 1] = behind + is_one * own
+        ahead, behind = around(p)
+        cross_out[p, 0] = ahead + oth + is_zero * own
+        cross_out[p, 1] = behind + oth + is_one * own
         return [send(cross_out.at[p], cross.at[p], cross_send.at[p], cross_recv.at[p], twin)]
 
     def inner(p, half, side, value):
@@ -265,10 +276,9 @@
 
     def own_inner(p):
         own, oth = grad[p, c], other[p]
-        ahead = back[p, :, 0].reshape(BLOCK, 256).astype(F32) + own + is_one * oth
-        behind = back[p, :, 1].reshape(BLOCK, 256).astype(F32) + own + is_zero * oth
-        centres[p, 0] = inner(p, c, 0, ahead)
-        centres[p, 1] = inner(p, c, 1, behind)
+        ahead, behind = around(p)
+        centres[p, 0] = inner(p, c, 0, ahead + own + is_one * oth)
+        centres[p, 1] = inner(p, c, 1, behind + own + is_zero * oth)
 
     def finish(p):
         query = qb[p].astype(F32)
@@ -283,6 +293,9 @@
     left, right, far = (s + 6) % 8, (s + 2) % 8, (s + 4) % 8
     given = [[], [], []]
 
+    def twin_slot(slot):
+        return slot + 1 - 2 * c
+
     def give(p, slot, k):
         given[p].append(send(kv.at[p, slot], kv.at[p, slot], core_send.at[p, k], core_recv.at[p, k], twin))
 
@@ -304,84 +317,109 @@
 
     lane = lax.broadcasted_iota(jnp.int32, (ROWS, 128), 1)
 
-    def attend(p):
+    near_slots = (s, twin_slot(s), left, twin_slot(left), right, twin_slot(right))
+    far_slots = (far, twin_slot(far))
+
+    def attend_half(p, half, slots, last):
         pair = qb[p]
-
-        def one(half):
-            query = jnp.where(lane // 64 == half, pair, jnp.zeros_like(pair))
-            top = None
-            for j in range(8):
-                block = nt(query, kv[p, j, 0])
-                scores[j] = block
-                peak = jnp.maximum(block[:, :128], block[:, 128:])
-                top = peak if top is None else jnp.maximum(top, peak)
-            top = jnp.max(top, axis=1, keepdims=True)
+        index = 2 * p + half
+        query = jnp.where(lane // 64 == half, pair, jnp.zeros_like(pair))
+        top = tops[index] if last else None
+        for k, slot in enumerate(slots):
+            block = nt(query, kv[p, slot, 0])
+            scores[k] = block
+            peak = jnp.maximum(block[:, :128], block[:, 128:])
+            top = peak if top is None else jnp.maximum(top, peak)
+        top = jnp.max(top, axis=1, keepdims=True)
+        if last:
+            fade = jnp.exp2((tops[index] - top) * SCALE)
+            total, summed = totals[index] * fade, sums[index] * fade
+        else:
             total = jnp.zeros((ROWS, 128), F32)
             summed = jnp.zeros((ROWS, 128), F32)
-            for j in range(8):
-                weight = jnp.exp2((scores[j] - top) * SCALE)
-                total = total + weight[:, :128] + weight[:, 128:]
-                summed = summed + nn(weight.astype(BF16), kv[p, j, 1])
-            return summed / jnp.sum(total, axis=1, keepdims=True)
-
-        first = one(0)
-        att[p] = jnp.where(lane < 64, first, one(1))
+        for k, slot in enumerate(slots):
+            weight = jnp.exp2((scores[k] - top) * SCALE)
+            total = total + weight[:, :128] + weight[:, 128:]
+            summed = summed + nn(weight.astype(BF16), kv[p, slot, 1])
+        if last:
+            summed = summed / jnp.sum(total, axis=1, keepdims=True)
+            att[p] = summed if half == 0 else jnp.where(lane < 64, att[p], summed)
+        else:
+            tops[index] = jnp.broadcast_to(top, (ROWS, 128))
+            totals[index] = total
+            sums[index] = summed
+
+    def attend_near(p, half):
+        attend_half(p, half, near_slots, False)
+
+    def attend_far(p):
+        for half in range(2):
+            attend_half(p, half, far_slots, True)
 
     wait(own_tokens[0] + tokens[0])
     hop0 = first_hop(0)
     gradients(0)
     swap0 = to_other_core(0)
     wait(own_tokens[1] + tokens[1])
+    hop1 = first_hop(1)
     gradients(1)
     swap1 = to_other_core(1)
     swap0.wait()
     chip0 = along_x(0)
-    hop1 = first_hop(1)
     wait(own_tokens[2] + tokens[2])
+    hop2 = first_hop(2)
     gradients(2)
     swap2 = to_other_core(2)
     swap1.wait()
     chip1 = along_x(1)
+    swap2.wait()
+    chip2 = along_x(2)
+    wait(hop0)
+    more0 = second_hop(0)
     wait(chip0)
     plane0 = along_z(0)
-    swap2.wait()
-    chip2 = along_x(2)
-    hop2 = first_hop(2)
-    wait(hop0)
-    more0 = second_hop(0)
     wait(chip1)
     plane1 = along_z(1)
     wait(chip2)
     plane2 = along_z(2)
+    wait(own_query + query_copies)
+    wait(given[0])
+    attend_near(0, 0)
+    attend_near(0, 1)
     wait(hop1)
     more1 = second_hop(1)
+    wait(plane0)
+    back0 = back_along_x(0)
+    wait(hop2)
+    more2 = second_hop(2)
+    wait(given[1])
+    attend_near(1, 0)
+    wait(plane1)
+    back1 = back_along_x(1)
+    attend_near(1, 1)
     wait(more0)
     give(0, far, 3)
-    wait(own_query + query_copies)
-    wait(given[0])
-    attend(0)
-    wait(hop2)
-    more2 = second_hop(2)
-    wait(plane0)
-    back0 = back_along_x(0)
+    wait(given[2])
+    attend_near(2, 0)
+    wait(plane2)
+    back2 = back_along_x(2)
     wait(more1)
     give(1, far, 3)
-    wait(plane1)
-    back1 = back_along_x(1)
-    wait(given[1])
-    attend(1)
-    wait(plane2)
-    back2 = back_along_x(2)
+    attend_near(2, 1)
     wait(more2)
     give(2, far, 3)
     wait(back0)
     cross0 = to_twin(0)
+    wait(given[0][3:])
+    attend_far(0)
     own_inner(0)
-    wait(given[2])
-    attend(2)
     wait(back1)
     cross1 = to_twin(1)
+    wait(given[1][3:])
+    attend_far(1)
     own_inner(1)
+    wait(given[2][3:])
+    attend_far(2)
     wait(cross0)
     finish(0)
     wait(back2)
@@ -414,13 +452,18 @@
         pltpu.VMEM((PAIRS, NX, PIECE, 256), CHIP_T),
         pltpu.VMEM((PAIRS, PIECE, 256), PLANE_T),
         pltpu.VMEM((PAIRS, NZ, PIECE, 256), PLANE_T),
-        pltpu.VMEM((PAIRS, NX, 2, PIECE, 256), BACK_T),
-        pltpu.VMEM((PAIRS, NX, 2, PIECE, 256), BACK_T),
+        pltpu.VMEM((PAIRS, NX, PIECE, 256), BF16),
+        pltpu.VMEM((PAIRS, NX, PIECE, 256), BF16),
+        pltpu.VMEM((PAIRS, PIECE, 256), F32),
+        pltpu.VMEM((PAIRS, NX, PIECE, 256), F32),
         pltpu.VMEM((PAIRS, 2, BLOCK, 256), F32),
         pltpu.VMEM((PAIRS, 2, BLOCK, 256), F32),
         pltpu.VMEM((PAIRS, 2, ROWS, 128), F32),
-        pltpu.VMEM((8, ROWS, 256), F32),
+        pltpu.VMEM((6, ROWS, 256), F32),
         pltpu.VMEM((PAIRS, ROWS, 128), F32),
+        pltpu.VMEM((HEADS, ROWS, 128), F32),
+        pltpu.VMEM((HEADS, ROWS, 128), F32),
+        pltpu.VMEM((HEADS, ROWS, 128), F32),
         dma((PAIRS, 3)),
         dma((2,)),
         dma((PAIRS, 2, NY)),
@@ -437,8 +480,8 @@
         dma((PAIRS, NX)),
         dma((PAIRS, NZ)),
         dma((PAIRS, NZ)),
-        dma((PAIRS, NX)),
-        dma((PAIRS, NX)),
+        dma((PAIRS, 2, NX)),
+        dma((PAIRS, 2, NX)),
         dma((PAIRS,)),
         dma((PAIRS,)),
     ]

time: 52.9 us -> 48.2 us (0.911)
  Pallas kernels: 51 us -> 46.2 us
    pallas_call x1, Pallas kernels: 51 us -> 46.2 us  [on_device(): pl.pallas_call(kernel, out_shape=jax.ShapeDtypeStruct((ROWS, WIDTH), F32)...]
where the time goes in v3:
time: 48.2 us; the launch traced here: 48 us
  Pallas kernels  46.2 us (96%)
  local copies, waits for them, and re-layouts  1.77 us (4%)
    pallas_call x1, Pallas kernels, on_device(): pl.pallas_call(kernel, out_shape=jax.ShapeDtypeStruct((ROWS, WIDTH), F32)...  46.2 us
    unnamed x1, local copies, waits for them, and re-layouts  1.77 us

profile of v3, /device:TPU:1, one launch (start us, length us, event | category | flops | bytes accessed | tf_op | source)
XLA Modules:
  0.0 48.0 jit_solution(13178824481253568028)
XLA Ops:
  0.0 46.2 %layer.1 = f32[256,384]{1,0:T(8,128)} custom-call(bf16[64,1536]{1,0:T(8,128)(2,1)} %q_hbm.1, bf16[64,1536]{1,0:T(8,128)(2,1)} %k_hbm.1, bf16[64,1536]{1,0:T(8,128)(2,1)} %v_hbm.1, f32[6,64,256]{2,1,0:T(8,128)} %w1_hbm.1, f32[6,64,256]{2,1,0:T(8,128)} %bitcast.1, f32[2,384]{1,0:T(2,128)} %gate_ref.1), custom_call_target="tpu_custom_call" | custom-call | tf_op jit(solution)/shard_map/layer/pallas_call | solution.py:488
  46.2 1.8 %copy.8 = f32[256,384]{1,0:T(8,128)} copy(f32[256,384]{1,0:T(8,128)} %layer.1) | data formatting | bytes 786432

commit v4 on v3

--- a/solution.py
+++ b/solution.py
@@ -376,22 +376,22 @@
     chip2 = along_x(2)
     wait(hop0)
     more0 = second_hop(0)
+    wait(hop1)
+    more1 = second_hop(1)
     wait(chip0)
     plane0 = along_z(0)
     wait(chip1)
     plane1 = along_z(1)
     wait(chip2)
     plane2 = along_z(2)
+    wait(hop2)
+    more2 = second_hop(2)
     wait(own_query + query_copies)
     wait(given[0])
     attend_near(0, 0)
     attend_near(0, 1)
-    wait(hop1)
-    more1 = second_hop(1)
     wait(plane0)
     back0 = back_along_x(0)
-    wait(hop2)
-    more2 = second_hop(2)
     wait(given[1])
     attend_near(1, 0)
     wait(plane1)

time: 48.2 us -> 47.2 us (0.979)
  Pallas kernels: 46.2 us -> 45.3 us
    pallas_call x1, Pallas kernels: 46.2 us -> 45.3 us  [on_device(): pl.pallas_call(kernel, out_shape=jax.ShapeDtypeStruct((ROWS, WIDTH), F32)...]
where the time goes in v4:
time: 47.2 us; the launch traced here: 47.1 us
  Pallas kernels  45.3 us (96%)
  local copies, waits for them, and re-layouts  1.77 us (4%)
    pallas_call x1, Pallas kernels, on_device(): pl.pallas_call(kernel, out_shape=jax.ShapeDtypeStruct((ROWS, WIDTH), F32)...  45.3 us
    unnamed x1, local copies, waits for them, and re-layouts  1.77 us

profile of v4, /device:TPU:1, one launch (start us, length us, event | category | flops | bytes accessed | tf_op | source)
XLA Modules:
  0.0 47.1 jit_solution(9204609958371543524)
XLA Ops:
  0.0 45.3 %layer.1 = f32[256,384]{1,0:T(8,128)} custom-call(bf16[64,1536]{1,0:T(8,128)(2,1)} %q_hbm.1, bf16[64,1536]{1,0:T(8,128)(2,1)} %k_hbm.1, bf16[64,1536]{1,0:T(8,128)(2,1)} %v_hbm.1, f32[6,64,256]{2,1,0:T(8,128)} %w1_hbm.1, f32[6,64,256]{2,1,0:T(8,128)} %bitcast.1, f32[2,384]{1,0:T(2,128)} %gate_ref.1), custom_call_target="tpu_custom_call" | custom-call | tf_op jit(solution)/shard_map/layer/pallas_call | solution.py:488
  45.3 1.8 %copy.8 = f32[256,384]{1,0:T(8,128)} copy(f32[256,384]{1,0:T(8,128)} %layer.1) | data formatting | bytes 786432

commit v5 on v4

--- a/solution.py
+++ b/solution.py
@@ -406,12 +406,12 @@
     wait(more1)
     give(1, far, 3)
     attend_near(2, 1)
+    wait(given[0][3:])
+    attend_far(0)
+    wait(back0)
+    cross0 = to_twin(0)
     wait(more2)
     give(2, far, 3)
-    wait(back0)
-    cross0 = to_twin(0)
-    wait(given[0][3:])
-    attend_far(0)
     own_inner(0)
     wait(back1)
     cross1 = to_twin(1)

time: 47.2 us -> 47 us (level)
  no operation moved by 1% of the time
where the time goes in v5:
time: 47 us; the launch traced here: 46.9 us
  Pallas kernels  45.1 us (96%)
  local copies, waits for them, and re-layouts  1.77 us (4%)
    pallas_call x1, Pallas kernels, on_device(): pl.pallas_call(kernel, out_shape=jax.ShapeDtypeStruct((ROWS, WIDTH), F32)...  45.1 us
    unnamed x1, local copies, waits for them, and re-layouts  1.77 us

profile of v5, /device:TPU:1, one launch (start us, length us, event | category | flops | bytes accessed | tf_op | source)
XLA Modules:
  0.0 46.9 jit_solution(5811402880373096410)
XLA Ops:
  0.0 45.1 %layer.1 = f32[256,384]{1,0:T(8,128)} custom-call(bf16[64,1536]{1,0:T(8,128)(2,1)} %q_hbm.1, bf16[64,1536]{1,0:T(8,128)(2,1)} %k_hbm.1, bf16[64,1536]{1,0:T(8,128)(2,1)} %v_hbm.1, f32[6,64,256]{2,1,0:T(8,128)} %w1_hbm.1, f32[6,64,256]{2,1,0:T(8,128)} %bitcast.1, f32[2,384]{1,0:T(2,128)} %gate_ref.1), custom_call_target="tpu_custom_call" | custom-call | tf_op jit(solution)/shard_map/layer/pallas_call | solution.py:488
  45.1 1.8 %copy.8 = f32[256,384]{1,0:T(8,128)} copy(f32[256,384]{1,0:T(8,128)} %layer.1) | data formatting | bytes 786432
